TPU v7x, 32 devices: a whole 2x2x4 slice. The times are simulated.
32 devices in a mesh: batch: 2 (over x), ctx: 16 (over z, y, core).
Axes of the slice: x: 2, y: 2, z: 4, core: 2. Of those that a mesh axis runs over, the one named last changes fastest.
Arguments:
- inputs: float32 [4, 1024, 768], P('batch', 'ctx'), may hold values from -6 to 6
- teacher: float32 [4, 1024, 768], P('batch', 'ctx'), may hold values from -6 to 6
- segments: int32 [4, 1024], P('batch'), may hold values from 0 to 15, never falling along the last dimension, each value on 1 to 768 neighbouring positions
- w_query: bfloat16 [768, 768], P('batch'), may hold values from -0.21875 to 0.21875
- b_query: bfloat16 [768], P('batch'), may hold values from -4 to 4
- w_key: bfloat16 [768, 768], P('batch'), may hold values from -0.21875 to 0.21875
- w_value: bfloat16 [768, 768], P('batch'), may hold values from -0.21875 to 0.21875
- b_value: bfloat16 [768], P('batch'), may hold values from -0.75 to 0.75
- w_out: bfloat16 [768, 768], P('batch'), may hold values from -1.25 to 1.25
- b_out: bfloat16 [768], P('batch'), may hold values from -4 to 4
- gain_one: bfloat16 [768], P('batch'), may hold values from 0.25 to 1.75
- shift_one: bfloat16 [768], P('batch'), may hold values from -4 to 4
- w_inner: bfloat16 [768, 3072], P('batch'), may hold values from -0.21875 to 0.21875
- b_inner: bfloat16 [3072], P('batch'), may hold values from -4 to 4
- w_outer: bfloat16 [3072, 768], P('batch'), may hold values from -0.109375 to 0.109375
- b_outer: bfloat16 [768], P('batch'), may hold values from -4 to 4
- gain_two: bfloat16 [768], P('batch'), may hold values from 0.25 to 1.75
- shift_two: bfloat16 [768], P('batch'), may hold values from -4 to 4
Outputs:
- output: float32 [4, 1024, 768], P('batch', 'ctx')
- loss: float32 [], replicated
- grad_inputs: float32 [4, 1024, 768], P('batch', 'ctx')
- grad_w_query: float32 [768, 768], P('batch')
- grad_b_query: float32 [768], P('batch')
- grad_w_key: float32 [768, 768], P('batch')
- grad_w_value: float32 [768, 768], P('batch')
- grad_b_value: float32 [768], P('batch')
- grad_w_out: float32 [768, 768], P('batch')
- grad_b_out: float32 [768], P('batch')
- grad_gain_one: float32 [768], P('batch')
- grad_shift_one: float32 [768], P('batch')
- grad_w_inner: float32 [768, 3072], P('batch')
- grad_b_inner: float32 [3072], P('batch')
- grad_w_outer: float32 [3072, 768], P('batch')
- grad_b_outer: float32 [768], P('batch')
- grad_gain_two: float32 [768], P('batch')
- grad_shift_two: float32 [768], P('batch')
Inputs may be any that keep to these rules, and one draw needn't show every extreme that they name: `segments`: segment ids never fall along a sequence, every id of 0 to 15 occurs in each sequence, each segment covers 1 to 768 positions and one covers exactly 768.
All inputs are finite; a program needn't handle non-finite values.
Results may differ from a plain program's by a relative error of at most 0.014.
The roundings to bfloat16 on the way count: a program that leaves them out, or rounds other values in their place, can miss the bound.
Values may be sent and summed in bfloat16 or wider, within the bound.
No kernel may reach another device: no remote copies, remote signals or barrier semaphores. Data moves between devices by JAX's collectives and lax.ppermute only.
A program may use at most 320 MiB of HBM per device.

v0:
```python
import jax
import jax.numpy as jnp
from jax import lax
from jax.sharding import PartitionSpec as P

H = 12
HD = 64
NEGATIVE = -1e30
EPSILON = 1e-12


def norm_rows(hidden, gain, shift):
    center = hidden - jnp.mean(hidden, -1, keepdims=True)
    spread = jnp.mean(center * center, -1, keepdims=True)
    return center * lax.rsqrt(spread + EPSILON) * gain + shift


def gelu_exact(values):
    return jax.nn.gelu(values, approximate=False)


def linear(rows_in, weight):
    return jnp.dot(rows_in, weight, preferred_element_type=jnp.float32)


def contract_rows(left, right):
    return lax.dot_general(
        left, right, (((0,), (0,)), ((), ())), preferred_element_type=jnp.float32
    )


def times_transpose(rows_in, weight):
    return lax.dot_general(
        rows_in, weight, (((1,), (1,)), ((), ())), preferred_element_type=jnp.float32
    )


def score_rows(query_one, keys_all, seg_mine, seg_all):
    heads_query = query_one.reshape(query_one.shape[0], H, HD)
    heads_key = keys_all.reshape(keys_all.shape[0], H, HD)
    raw = jnp.einsum(
        "chd,khd->hck", heads_query, heads_key, preferred_element_type=jnp.float32
    ) * HD ** (-0.5)
    allowed = seg_mine[None, :, None] == seg_all[None, None, :]
    return jnp.where(allowed, raw, NEGATIVE)


def per_device(
    inputs,
    teacher,
    segments,
    w_query,
    b_query,
    w_key,
    w_value,
    b_value,
    w_out,
    b_out,
    gain_one,
    shift_one,
    w_inner,
    b_inner,
    w_outer,
    b_outer,
    gain_two,
    shift_two,
):
    (
        w_query,
        b_query,
        w_key,
        w_value,
        b_value,
        w_out,
        b_out,
        gain_one,
        shift_one,
        w_inner,
        b_inner,
        w_outer,
        b_outer,
        gain_two,
        shift_two,
    ) = (
        lax.all_gather(w_query, "batch", axis=0, tiled=True),
        lax.all_gather(b_query, "batch", axis=0, tiled=True),
        lax.all_gather(w_key, "batch", axis=0, tiled=True),
        lax.all_gather(w_value, "batch", axis=0, tiled=True),
        lax.all_gather(b_value, "batch", axis=0, tiled=True),
        lax.all_gather(w_out, "batch", axis=0, tiled=True),
        lax.all_gather(b_out, "batch", axis=0, tiled=True),
        lax.all_gather(gain_one, "batch", axis=0, tiled=True),
        lax.all_gather(shift_one, "batch", axis=0, tiled=True),
        lax.all_gather(w_inner, "batch", axis=0, tiled=True),
        lax.all_gather(b_inner, "batch", axis=0, tiled=True),
        lax.all_gather(w_outer, "batch", axis=0, tiled=True),
        lax.all_gather(b_outer, "batch", axis=0, tiled=True),
        lax.all_gather(gain_two, "batch", axis=0, tiled=True),
        lax.all_gather(shift_two, "batch", axis=0, tiled=True),
    )
    scale = HD ** (-0.5)
    seqs_here, ctx_rows, width = inputs.shape
    rows_here = seqs_here * ctx_rows
    tokens_all = rows_here * lax.axis_size("batch") * lax.axis_size("ctx")
    seg_own = lax.dynamic_slice_in_dim(segments, lax.axis_index("ctx") * ctx_rows, ctx_rows, 1)
    inputs_flat = inputs.reshape(rows_here, width)
    inputs_low = inputs_flat.astype(jnp.bfloat16)
    query = (linear(inputs_low, w_query) + b_query.astype(jnp.float32)).astype(jnp.bfloat16)
    key = linear(inputs_low, w_key).astype(jnp.bfloat16)
    value = (linear(inputs_low, w_value) + b_value.astype(jnp.float32)).astype(jnp.bfloat16)
    query_seq = query.reshape(seqs_here, ctx_rows, width)
    key_seq = key.reshape(seqs_here, ctx_rows, width)
    value_seq = value.reshape(seqs_here, ctx_rows, width)

    def attend_forward(items):
        query_one, key_one, value_one, seg_all, seg_mine = items
        keys_all, values_all = (
            lax.all_gather(key_one, "ctx", axis=0, tiled=True),
            lax.all_gather(value_one, "ctx", axis=0, tiled=True),
        )
        scores = score_rows(query_one, keys_all, seg_mine, seg_all)
        highest = jnp.max(scores, -1, keepdims=True)
        expo = jnp.exp(scores - highest)
        totals = jnp.sum(expo, -1, keepdims=True)
        probs = (expo / totals).astype(jnp.bfloat16)
        mixed = jnp.einsum(
            "hck,khd->chd",
            probs,
            values_all.reshape(keys_all.shape[0], H, HD),
            preferred_element_type=jnp.float32,
        )
        return (
            mixed.reshape(ctx_rows, width).astype(jnp.bfloat16),
            (highest + jnp.log(totals))[:, :, 0],
        )

    attended, log_totals = lax.map(
        attend_forward, (query_seq, key_seq, value_seq, segments, seg_own)
    )
    attended_flat = attended.reshape(rows_here, width)
    gain_one_full = gain_one.astype(jnp.float32)
    shift_one_full = shift_one.astype(jnp.float32)
    gain_two_full = gain_two.astype(jnp.float32)
    shift_two_full = shift_two.astype(jnp.float32)
    hidden_one = inputs_flat + linear(attended_flat, w_out) + b_out.astype(jnp.float32)
    normed_one, back_one = jax.vjp(norm_rows, hidden_one, gain_one_full, shift_one_full)
    normed_low = normed_one.astype(jnp.bfloat16)
    inner_pre = linear(normed_low, w_inner) + b_inner.astype(jnp.float32)
    active_full, gelu_back = jax.vjp(gelu_exact, inner_pre)
    active_low = active_full.astype(jnp.bfloat16)
    hidden_two = normed_one + linear(active_low, w_outer) + b_outer.astype(jnp.float32)
    output, back_two = jax.vjp(norm_rows, hidden_two, gain_two_full, shift_two_full)
    valid = (seg_own.reshape(rows_here) != 0).astype(jnp.float32)[:, None]
    error = output - teacher.reshape(rows_here, width)
    loss_total, valid_count = lax.psum(
        (jnp.sum(valid * error * error), jnp.sum(valid)), ("batch", "ctx")
    )
    loss = loss_total / (2.0 * valid_count)
    grad_output = tokens_all / valid_count * valid * error
    grad_hidden_two, grad_gain_two, grad_shift_two = back_two(grad_output)
    grad_branch_two = grad_hidden_two.astype(jnp.bfloat16)
    grad_b_outer = jnp.sum(grad_branch_two.astype(jnp.float32), 0)
    grad_w_outer = contract_rows(active_low, grad_branch_two)
    grad_active = times_transpose(grad_branch_two, w_outer)
    grad_inner = gelu_back(grad_active)[0].astype(jnp.bfloat16)
    grad_b_inner = jnp.sum(grad_inner.astype(jnp.float32), 0)
    grad_w_inner = contract_rows(normed_low, grad_inner)
    grad_normed = grad_hidden_two + times_transpose(grad_inner, w_inner)
    grad_hidden_one, grad_gain_one, grad_shift_one = back_one(grad_normed)
    grad_branch_one = grad_hidden_one.astype(jnp.bfloat16)
    grad_b_out = jnp.sum(grad_branch_one.astype(jnp.float32), 0)
    grad_w_out = contract_rows(attended_flat, grad_branch_one)
    grad_attended = (
        times_transpose(grad_branch_one, w_out)
        .astype(jnp.bfloat16)
        .reshape(seqs_here, ctx_rows, width)
    )

    def attend_backward(items):
        query_one, key_one, value_one, seg_all, seg_mine, log_one, grad_one = items
        keys_all, values_all = (
            lax.all_gather(key_one, "ctx", axis=0, tiled=True),
            lax.all_gather(value_one, "ctx", axis=0, tiled=True),
        )
        key_count = keys_all.shape[0]
        scores = score_rows(query_one, keys_all, seg_mine, seg_all)
        probs = jnp.exp(scores - log_one[:, :, None])
        grad_heads = grad_one.reshape(ctx_rows, H, HD)
        grad_probs = jnp.einsum(
            "chd,khd->hck",
            grad_heads,
            values_all.reshape(key_count, H, HD),
            preferred_element_type=jnp.float32,
        )
        centre = jnp.sum(probs * grad_probs, -1)
        grad_scores = (probs * (grad_probs - centre[:, :, None])).astype(jnp.bfloat16)
        grad_query = (
            jnp.einsum(
                "hck,khd->chd",
                grad_scores,
                keys_all.reshape(key_count, H, HD),
                preferred_element_type=jnp.float32,
            )
            * scale
        )
        grad_query = grad_query.reshape(ctx_rows, width).astype(jnp.bfloat16)
        probs_low = probs.astype(jnp.bfloat16)
        query_heads = query_one.reshape(ctx_rows, H, HD)
        count = ctx_rows * lax.axis_size("ctx")
        grad_key = (
            jnp.einsum("hck,chd->khd", grad_scores, query_heads, preferred_element_type=jnp.float32)
            * scale
        )
        grad_value = jnp.einsum(
            "hck,chd->khd", probs_low, grad_heads, preferred_element_type=jnp.float32
        )
        both = lax.psum_scatter(
            jnp.concatenate([grad_key.reshape(count, width), grad_value.reshape(count, width)], 1),
            "ctx",
            scatter_dimension=0,
            tiled=True,
        )
        return (
            grad_query,
            both[:, :width].astype(jnp.bfloat16),
            both[:, width:].astype(jnp.bfloat16),
        )

    grad_query_seq, grad_key_seq, grad_value_seq = lax.map(
        attend_backward,
        (query_seq, key_seq, value_seq, segments, seg_own, log_totals, grad_attended),
    )
    grad_query_flat = grad_query_seq.reshape(rows_here, width)
    grad_key_flat = grad_key_seq.reshape(rows_here, width)
    grad_value_flat = grad_value_seq.reshape(rows_here, width)
    grad_w_query = contract_rows(inputs_low, grad_query_flat)
    grad_b_query = jnp.sum(grad_query_flat.astype(jnp.float32), 0)
    grad_w_key = contract_rows(inputs_low, grad_key_flat)
    grad_w_value = contract_rows(inputs_low, grad_value_flat)
    grad_b_value = jnp.sum(grad_value_flat.astype(jnp.float32), 0)
    grad_inputs = (
        grad_hidden_one
        + times_transpose(grad_query_flat, w_query)
        + times_transpose(grad_key_flat, w_key)
        + times_transpose(grad_value_flat, w_value)
    )
    (
        grad_w_query,
        grad_b_query,
        grad_w_key,
        grad_w_value,
        grad_b_value,
        grad_w_out,
        grad_b_out,
        grad_gain_one,
        grad_shift_one,
        grad_w_inner,
        grad_b_inner,
        grad_w_outer,
        grad_b_outer,
        grad_gain_two,
        grad_shift_two,
    ) = (
        lax.psum_scatter(
            grad_w_query.astype(jnp.bfloat16), "batch", scatter_dimension=0, tiled=True
        ).astype(jnp.float32),
        lax.psum_scatter(
            grad_b_query.astype(jnp.bfloat16), "batch", scatter_dimension=0, tiled=True
        ).astype(jnp.float32),
        lax.psum_scatter(
            grad_w_key.astype(jnp.bfloat16), "batch", scatter_dimension=0, tiled=True
        ).astype(jnp.float32),
        lax.psum_scatter(
            grad_w_value.astype(jnp.bfloat16), "batch", scatter_dimension=0, tiled=True
        ).astype(jnp.float32),
        lax.psum_scatter(
            grad_b_value.astype(jnp.bfloat16), "batch", scatter_dimension=0, tiled=True
        ).astype(jnp.float32),
        lax.psum_scatter(
            grad_w_out.astype(jnp.bfloat16), "batch", scatter_dimension=0, tiled=True
        ).astype(jnp.float32),
        lax.psum_scatter(
            grad_b_out.astype(jnp.bfloat16), "batch", scatter_dimension=0, tiled=True
        ).astype(jnp.float32),
        lax.psum_scatter(
            grad_gain_one.astype(jnp.bfloat16), "batch", scatter_dimension=0, tiled=True
        ).astype(jnp.float32),
        lax.psum_scatter(
            grad_shift_one.astype(jnp.bfloat16), "batch", scatter_dimension=0, tiled=True
        ).astype(jnp.float32),
        lax.psum_scatter(
            grad_w_inner.astype(jnp.bfloat16), "batch", scatter_dimension=0, tiled=True
        ).astype(jnp.float32),
        lax.psum_scatter(
            grad_b_inner.astype(jnp.bfloat16), "batch", scatter_dimension=0, tiled=True
        ).astype(jnp.float32),
        lax.psum_scatter(
            grad_w_outer.astype(jnp.bfloat16), "batch", scatter_dimension=0, tiled=True
        ).astype(jnp.float32),
        lax.psum_scatter(
            grad_b_outer.astype(jnp.bfloat16), "batch", scatter_dimension=0, tiled=True
        ).astype(jnp.float32),
        lax.psum_scatter(
            grad_gain_two.astype(jnp.bfloat16), "batch", scatter_dimension=0, tiled=True
        ).astype(jnp.float32),
        lax.psum_scatter(
            grad_shift_two.astype(jnp.bfloat16), "batch", scatter_dimension=0, tiled=True
        ).astype(jnp.float32),
    )
    (
        grad_w_query,
        grad_b_query,
        grad_w_key,
        grad_w_value,
        grad_b_value,
        grad_w_out,
        grad_b_out,
        grad_gain_one,
        grad_shift_one,
        grad_w_inner,
        grad_b_inner,
        grad_w_outer,
        grad_b_outer,
        grad_gain_two,
        grad_shift_two,
    ) = lax.psum(
        (
            grad_w_query,
            grad_b_query,
            grad_w_key,
            grad_w_value,
            grad_b_value,
            grad_w_out,
            grad_b_out,
            grad_gain_one,
            grad_shift_one,
            grad_w_inner,
            grad_b_inner,
            grad_w_outer,
            grad_b_outer,
            grad_gain_two,
            grad_shift_two,
        ),
        "ctx",
    )
    return (
        output.reshape(inputs.shape),
        loss,
        grad_inputs.reshape(inputs.shape),
        grad_w_query,
        grad_b_query,
        grad_w_key,
        grad_w_value,
        grad_b_value,
        grad_w_out,
        grad_b_out,
        grad_gain_one,
        grad_shift_one,
        grad_w_inner,
        grad_b_inner,
        grad_w_outer,
        grad_b_outer,
        grad_gain_two,
        grad_shift_two,
    )


def solution(mesh):
    placed = (
        P("batch", "ctx", None),
        P("batch", "ctx", None),
        P("batch", None),
        P("batch", None),
        P("batch"),
        P("batch", None),
        P("batch", None),
        P("batch"),
        P("batch", None),
        P("batch"),
        P("batch"),
        P("batch"),
        P("batch", None),
        P("batch"),
        P("batch", None),
        P("batch"),
        P("batch"),
        P("batch"),
    )
    return jax.shard_map(
        per_device,
        mesh=mesh,
        in_specs=placed,
        out_specs=(
            P("batch", "ctx", None),
            P(),
            P("batch", "ctx", None),
            P("batch", None),
            P("batch"),
            P("batch", None),
            P("batch", None),
            P("batch"),
            P("batch", None),
            P("batch"),
            P("batch"),
            P("batch"),
            P("batch", None),
            P("batch"),
            P("batch", None),
            P("batch"),
            P("batch"),
            P("batch"),
        ),
        check_vma=False,
    )
```

profile of v0, /device:TPU:1, one launch (start us, length us, event | category | flops | bytes accessed | tf_op | source)
XLA Modules:
  0.0 1352.9 jit_solution(5243858806981145889)
XLA Ops:
  9.5 3.7 all-gather.5
  13.3 3.2 all-gather.4
  17.3 17.2 %all-gather.36.cloned.1.call-done = bf16[768,768]{1,0:T(8,128)(2,1)} async-done(((bf16[384,768]{1,0:T(8,128)(2,1)}), bf16[768,768]{1,0:T(8,128)(2,1)}) %all-gather.36.cloned.1.call-update) | async-done | bytes 1179664 | tf_op jit(solution)/shard_map/all_gather | solution.py:87
  34.5 2.3 convolution_convert_fusion.4
  36.8 22.1 %all-gather.34.cloned.1.call-done = bf16[768,768]{1,0:T(8,128)(2,1)} async-done(((bf16[384,768]{1,0:T(8,128)(2,1)}), bf16[768,768]{1,0:T(8,128)(2,1)}) %all-gather.34.cloned.1.call-update) | async-done | bytes 1179664 | tf_op jit(solution)/shard_map/all_gather | solution.py:85
  58.8 2.3 fusion.27
  61.1 22.1 %all-gather.32.cloned.1.call-done = bf16[768,768]{1,0:T(8,128)(2,1)} async-done(((bf16[384,768]{1,0:T(8,128)(2,1)}), bf16[768,768]{1,0:T(8,128)(2,1)}) %all-gather.32.cloned.1.call-update) | async-done | bytes 1179664 | tf_op jit(solution)/shard_map/all_gather | solution.py:88
  83.2 2.3 fusion.26
  85.5 181.2 %while.26 = (s32[]{:T(128)}, bf16[2,64,768]{2,1,0:T(8,128)(2,1)}, f32[2,12,64]{2,1,0:T(8,128)}, bf16[2,64,768]{2,1,0:T(8,128)(2,1)}, s32[2,64]{1,0:T(2,128)S(1)}...) while((s32[]{:T(128)}, bf16[2,64,768]{2,1,0:T(8,128)(2,1)}, ...), condition=%wide.region_3.4_spmd, body=%wide.region_0.3_spmd.sunk | while | flops 210877696 | bytes 30582736 | solution.py:137
  90.6 38.4 %all-gather.46.cloned.1.call-done = bf16[1,1024,768]{2,1,0:T(8,128)(2,1)} async-done(((bf16[1,64,768]{2,1,0:T(8,128)(2,1)}), bf16[1,1024,768]{2,1,0:T(8,128)(2,1)}) %all-gather.46.cloned.1.call-update) | async-done | bytes 1572880 | tf_op jit(solution)/shard_map/while/body/eval_jaxpr/all_gather | solution.py:118
  129.0 2.6 copy.122
  131.6 2.2 fusion.113
  134.6 35.7 %all-gather.44.cloned.1.call-done = bf16[1,1024,768]{2,1,0:T(8,128)(2,1)} async-done(((bf16[1,64,768]{2,1,0:T(8,128)(2,1)}), bf16[1,1024,768]{2,1,0:T(8,128)(2,1)}) %all-gather.44.cloned.1.call-update) | async-done | bytes 1572880 | tf_op jit(solution)/shard_map/while/body/eval_jaxpr/all_gather | solution.py:119
  170.3 2.6 copy.121
  172.9 2.5 fusion.115
  181.9 36.9 %all-gather.46.cloned.1.call-done = bf16[1,1024,768]{2,1,0:T(8,128)(2,1)} async-done(((bf16[1,64,768]{2,1,0:T(8,128)(2,1)}), bf16[1,1024,768]{2,1,0:T(8,128)(2,1)}) %all-gather.46.cloned.1.call-update) | async-done | bytes 1572880 | tf_op jit(solution)/shard_map/while/body/eval_jaxpr/all_gather | solution.py:118
  218.7 2.6 copy.122
  221.3 2.2 fusion.113
  224.4 35.8 %all-gather.44.cloned.1.call-done = bf16[1,1024,768]{2,1,0:T(8,128)(2,1)} async-done(((bf16[1,64,768]{2,1,0:T(8,128)(2,1)}), bf16[1,1024,768]{2,1,0:T(8,128)(2,1)}) %all-gather.44.cloned.1.call-update) | async-done | bytes 1572880 | tf_op jit(solution)/shard_map/while/body/eval_jaxpr/all_gather | solution.py:119
  260.2 2.6 copy.121
  262.8 2.5 fusion.115
  269.5 38.7 %psum.120 = f32[]{:T(128)} all-reduce(f32[]{:T(128)} %convert_reduce_fusion.8), channel_id=1, replica_groups=mesh['batch'=2,'ctx'=16] {'batch','ctx'}, use_global_device_ids=true, to_apply=%region_11.12 | all-reduce | flops 1 | bytes 8 | tf_op jit(solution)/shard_map/psum | solution.py:155
  308.2 3.5 all-gather.6
  311.8 3.5 all-gather.7
  315.3 3.5 all-gather.8
  318.9 3.5 all-gather.10
  322.5 3.5 all-gather.11
  326.0 3.5 all-gather.12
  330.4 3.8 all-gather.9
  336.3 19.3 %all-gather.40.cloned.1.call-done = bf16[768,3072]{1,0:T(8,128)(2,1)} async-done(((bf16[384,3072]{1,0:T(8,128)(2,1)}), bf16[768,3072]{1,0:T(8,128)(2,1)}) %all-gather.40.cloned.1.call-update) | async-done | bytes 4718608 | tf_op jit(solution)/shard_map/all_gather | solution.py:94
  355.6 7.6 multiply_convert_fusion.1
  363.2 56.3 %all-gather.42.cloned.1.call-done = bf16[3072,768]{1,0:T(8,128)(2,1)} async-done(((bf16[1536,768]{1,0:T(8,128)(2,1)}), bf16[3072,768]{1,0:T(8,128)(2,1)}) %all-gather.42.cloned.1.call-update) | async-done | bytes 4718608 | tf_op jit(solution)/shard_map/all_gather | solution.py:96
  419.5 3.4 fusion.45
  425.7 2.5 fusion.39
  428.2 2.4 multiply_reduce_fusion.2
  433.6 376.0 %while.27 = (s32[]{:T(128)}, bf16[2,64,768]{1,2,0:T(8,128)(2,1)}, bf16[2,64,768]{1,2,0:T(8,128)(2,1)}, bf16[2,64,768]{1,2,0:T(8,128)(2,1)}, bf16[2,64,768]{2,1,0...) while((s32[]{:T(128)}, bf16[2,64,768]{1,2,0:T(8,128)(2,1)}, ...), condition=%wide.region_19.20_spmd, body=%wide.region_16.19_spmd.sunk | while | flops 512916736 | bytes 120094944 | solution.py:229
  440.3 37.1 %all-gather.50.cloned.1.call-done = bf16[1,1024,768]{2,1,0:T(8,128)(2,1)} async-done(((bf16[1,64,768]{2,1,0:T(8,128)(2,1)}), bf16[1,1024,768]{2,1,0:T(8,128)(2,1)}) %all-gather.50.cloned.1.call-update) | async-done | bytes 1572880 | tf_op jit(solution)/shard_map/while/body/eval_jaxpr/all_gather | solution.py:183
  477.4 2.6 copy.126
  480.0 2.0 fusion.126
  482.0 36.7 %all-gather.48.cloned.1.call-done = bf16[1,1024,768]{2,1,0:T(8,128)(2,1)} async-done(((bf16[1,64,768]{2,1,0:T(8,128)(2,1)}), bf16[1,1024,768]{2,1,0:T(8,128)(2,1)}) %all-gather.48.cloned.1.call-update) | async-done | bytes 1572880 | tf_op jit(solution)/shard_map/while/body/eval_jaxpr/all_gather | solution.py:182
  518.7 2.6 copy.124
  521.3 2.8 multiply_reduce_fusion.9
  526.1 3.2 pad_maximum_fusion.2
  529.4 6.6 copy.128
  539.1 80.0 %reduce-scatter.30.cloned.1.call-done = f32[64,1536]{1,0:T(8,128)} async-done(((f32[1024,1536]{1,0:T(8,128)}), f32[64,1536]{1,0:T(8,128)}) %reduce-scatter.30.cloned.1.call-update) | async-done | bytes 393232 | tf_op jit(solution)/shard_map/while
  628.5 36.6 %all-gather.50.cloned.1.call-done = bf16[1,1024,768]{2,1,0:T(8,128)(2,1)} async-done(((bf16[1,64,768]{2,1,0:T(8,128)(2,1)}), bf16[1,1024,768]{2,1,0:T(8,128)(2,1)}) %all-gather.50.cloned.1.call-update) | async-done | bytes 1572880 | tf_op jit(solution)/shard_map/while/body/eval_jaxpr/all_gather | solution.py:183
  665.2 2.6 copy.126
  667.7 2.0 fusion.126
  669.8 36.7 %all-gather.48.cloned.1.call-done = bf16[1,1024,768]{2,1,0:T(8,128)(2,1)} async-done(((bf16[1,64,768]{2,1,0:T(8,128)(2,1)}), bf16[1,1024,768]{2,1,0:T(8,128)(2,1)}) %all-gather.48.cloned.1.call-update) | async-done | bytes 1572880 | tf_op jit(solution)/shard_map/while/body/eval_jaxpr/all_gather | solution.py:182
  706.5 2.6 copy.124
  709.0 2.8 multiply_reduce_fusion.9
  713.9 3.2 pad_maximum_fusion.2
  717.1 6.6 copy.128
  726.9 80.0 %reduce-scatter.30.cloned.1.call-done = f32[64,1536]{1,0:T(8,128)} async-done(((f32[1024,1536]{1,0:T(8,128)}), f32[64,1536]{1,0:T(8,128)}) %reduce-scatter.30.cloned.1.call-update) | async-done | bytes 393232 | tf_op jit(solution)/shard_map/while
  818.6 3.7 convolution_convert_fusion.1
  823.4 3.6 convolution_convert_fusion
  830.2 39.9 %psum.119 = f32[]{:T(128)} all-reduce(f32[]{:T(128)} %get-tuple-element.222), channel_id=1, replica_groups=mesh['batch'=2,'ctx'=16] {'batch','ctx'}, use_global_device_ids=true, to_apply=%region_9.10 | all-reduce | flops 1 | bytes 8 | tf_op jit(solution)/shard_map/psum | solution.py:155
  870.9 1.8 reduce_sum.246
  875.7 7.7 all-reduce.10
  891.6 17.3 %reduce-scatter.18.cloned.1.call-done = bf16[384,768]{1,0:T(8,128)(2,1)} async-done(((bf16[768,768]{1,0:T(8,128)(2,1)}), bf16[384,768]{1,0:T(8,128)(2,1)}) %reduce-scatter.18.cloned.1.call-update) | async-done | bytes 589840 | tf_op jit(solution)/shard_map/reduce_scatter | solution.py:279
  908.9 62.9 %reduce-scatter.20.cloned.1.call-done = bf16[384,3072]{1,0:T(8,128)(2,1)} async-done(((bf16[768,3072]{1,0:T(8,128)(2,1)}), bf16[384,3072]{1,0:T(8,128)(2,1)}) %reduce-scatter.20.cloned.1.call-update) | async-done | bytes 2359312 | tf_op jit(solution)/shard_map/reduce_scatter | solution.py:291
  971.8 63.0 %reduce-scatter.22.cloned.1.call-done = bf16[1536,768]{1,0:T(8,128)(2,1)} async-done(((bf16[3072,768]{1,0:T(8,128)(2,1)}), bf16[1536,768]{1,0:T(8,128)(2,1)}) %reduce-scatter.22.cloned.1.call-update) | async-done | bytes 2359312 | tf_op jit(solution)/shard_map/reduce_scatter | solution.py:297
  1034.8 304.6 %all-reduce.12 = (f32[384,768]{0,1:T(8,128)}, f32[384]{0:T(512)}, f32[384,768]{0,1:T(8,128)}, f32[384,768]{0,1:T(8,128)S(1)}, f32[384]{0:T(512)}, /*index=5*/f32...) all-reduce(bf16[384,768]{0,1:T(8,128)(2,1)S(1)} %copy.92, ...), channel_id=1, replica_groups=mesh['batch'=2,'ctx'=16] {'ctx'}, use_global_device_ids=true, to_apply=%region_21.22 | all-reduce | flops 3543552 | bytes 21270528 | tf_op jit(solution)/shard_map/psum | solution.py:326
  1339.4 2.7 copy.83
  (308 shorter events, 82.5 us)
Async XLA Ops:
  7.2 2.3 copy-start.44
  7.2 6.1 copy-start.45
  7.2 10.0 copy-start.5
  7.2 27.3 %all-gather.36.cloned.1.call-start = ((), (), s32[]{:S(2)}) async-start(), calls=%async_computation.9 | async-start | bytes 1769472 | tf_op jit(solution)/shard_map/all_gather | solution.py:87
  8.0 50.9 %all-gather.34.cloned.1.call-start = ((), (), s32[]{:S(2)}) async-start(), calls=%async_computation.8 | async-start | bytes 1769472 | tf_op jit(solution)/shard_map/all_gather | solution.py:85
  8.7 74.5 %all-gather.32.cloned.1.call-start = ((), (), s32[]{:S(2)}) async-start(), calls=%async_computation.7 | async-start | bytes 1769472 | tf_op jit(solution)/shard_map/all_gather | solution.py:88
  85.5 43.5 %all-gather.46.cloned.1.call-start = ((), (), s32[]{:S(2)}) async-start(), calls=%async_computation.20 | async-start | bytes 1671168 | tf_op jit(solution)/shard_map/while/body/eval_jaxpr/all_gather | solution.py:118
  87.1 83.2 %all-gather.44.cloned.1.call-start = ((), (), s32[]{:S(2)}) async-start(), calls=%async_computation.19 | async-start | bytes 1671168 | tf_op jit(solution)/shard_map/while/body/eval_jaxpr/all_gather | solution.py:119
  176.8 42.0 %all-gather.46.cloned.1.call-start = ((), (), s32[]{:S(2)}) async-start(), calls=%async_computation.20 | async-start | bytes 1671168 | tf_op jit(solution)/shard_map/while/body/eval_jaxpr/all_gather | solution.py:118
  178.3 81.8 %all-gather.44.cloned.1.call-start = ((), (), s32[]{:S(2)}) async-start(), calls=%async_computation.19 | async-start | bytes 1671168 | tf_op jit(solution)/shard_map/while/body/eval_jaxpr/all_gather | solution.py:119
  266.7 67.6 %all-gather.38.cloned.1.call-start = ((), (), s32[]{:S(2)}) async-start(), calls=%async_computation.10 | async-start | bytes 1769472 | tf_op jit(solution)/shard_map/all_gather | solution.py:90
  267.4 88.2 %all-gather.40.cloned.1.call-start = ((), (), s32[]{:S(2)}) async-start(), calls=%async_computation.11 | async-start | bytes 7077888 | tf_op jit(solution)/shard_map/all_gather | solution.py:94
  268.2 40.0 %copy-start.46 = (bf16[384]{0:T(512)(128)(2,1)S(1)}, bf16[384]{0:T(512)(128)(2,1)}, u32[]{:S(2)}) copy-start(bf16[384]{0:T(512)(128)(2,1)} %param.31) | copy-start | bytes 2308
  268.2 43.6 %copy-start.47 = (bf16[384]{0:T(512)(128)(2,1)S(1)}, bf16[384]{0:T(512)(128)(2,1)}, u32[]{:S(2)}) copy-start(bf16[384]{0:T(512)(128)(2,1)} %param.32) | copy-start | bytes 2308
  268.2 47.1 %copy-start.48 = (bf16[384]{0:T(512)(128)(2,1)S(1)}, bf16[384]{0:T(512)(128)(2,1)}, u32[]{:S(2)}) copy-start(bf16[384]{0:T(512)(128)(2,1)} %param.33) | copy-start | bytes 2308
  268.2 50.7 %copy-start.49 = (bf16[384]{0:T(512)(128)(2,1)S(1)}, bf16[384]{0:T(512)(128)(2,1)}, u32[]{:S(2)}) copy-start(bf16[384]{0:T(512)(128)(2,1)} %param.37) | copy-start | bytes 2308
  268.2 54.2 %copy-start.50 = (bf16[384]{0:T(512)(128)(2,1)S(1)}, bf16[384]{0:T(512)(128)(2,1)}, u32[]{:S(2)}) copy-start(bf16[384]{0:T(512)(128)(2,1)} %param.38) | copy-start | bytes 2308
  268.2 57.8 %copy-start.51 = (bf16[384]{0:T(512)(128)(2,1)S(1)}, bf16[384]{0:T(512)(128)(2,1)}, u32[]{:S(2)}) copy-start(bf16[384]{0:T(512)(128)(2,1)} %param.39) | copy-start | bytes 2308
  268.2 62.2 %copy-start.42 = (bf16[1536]{0:T(1024)(128)(2,1)S(1)}, bf16[1536]{0:T(1024)(128)(2,1)}, u32[]{:S(2)}) copy-start(bf16[1536]{0:T(1024)(128)(2,1)} %param.35) | copy-start | bytes 9220
  268.2 66.1 %copy-start.6 = (f32[2,64,768]{2,1,0:T(8,128)S(1)}, f32[2,64,768]{2,1,0:T(8,128)}, u32[]{:S(2)}) copy-start(f32[2,64,768]{2,1,0:T(8,128)} %param.22) | copy-start | bytes 1179652
  268.3 66.1 %copy-start.26 = (bf16[2,64,768]{2,1,0:T(8,128)(2,1)S(1)}, bf16[2,64,768]{2,1,0:T(8,128)(2,1)}, u32[]{:S(2)}) copy-start(bf16[2,64,768]{2,1,0:T(8,128)(2,1)} %get-tuple-element.120) | copy-start | bytes 589828
  268.3 151.2 %all-gather.42.cloned.1.call-start = ((), (), s32[]{:S(2)}) async-start(), calls=%async_computation.12 | async-start | bytes 7077888 | tf_op jit(solution)/shard_map/all_gather | solution.py:96
  336.0 94.6 %copy-start.3 = (f32[128,768]{1,0:T(8,128)}, f32[128,768]{1,0:T(8,128)S(1)}, u32[]{:S(2)}) copy-start(f32[128,768]{1,0:T(8,128)S(1)} %get-tuple-element.311) | copy-start | bytes 1179652
  336.0 94.6 %copy-start.32 = (f32[128]{0:T(128)}, f32[128]{0:T(128)S(1)}, u32[]{:S(2)}) copy-start(f32[128]{0:T(128)S(1)} %broadcast_multiply_fusion.1) | copy-start | bytes 1540
  336.3 94.4 %copy-start.34 = (f32[128]{0:T(128)}, f32[128]{0:T(128)S(1)}, u32[]{:S(2)}) copy-start(f32[128]{0:T(128)S(1)} %fusion.30) | copy-start | bytes 1540
  363.2 59.7 %copy-start.8 = (bf16[128,3072]{1,0:T(8,128)(2,1)}, bf16[128,3072]{1,0:T(8,128)(2,1)S(1)}, u32[]{:S(2)}) copy-start(bf16[128,3072]{1,0:T(8,128)(2,1)S(1)} %get-tuple-element.300) | copy-start | bytes 2359300
  419.5 3.6 copy-start.31
  419.5 6.2 copy-start.10
  423.1 2.6 copy-start.53
  424.8 3.5 slice-start
  425.7 2.5 copy-start.29
  425.7 2.5 slice-start.1
  428.2 2.4 copy-start.20
  430.6 1.7 copy-start.14
  430.9 2.7 copy-start.43
  433.6 5.3 copy-start.40
  433.6 43.8 %all-gather.50.cloned.1.call-start = ((), (), s32[]{:S(2)}) async-start(), calls=%async_computation.22 | async-start | bytes 1671168 | tf_op jit(solution)/shard_map/while/body/eval_jaxpr/all_gather | solution.py:183
  435.2 83.5 %all-gather.48.cloned.1.call-start = ((), (), s32[]{:S(2)}) async-start(), calls=%async_computation.21 | async-start | bytes 1671168 | tf_op jit(solution)/shard_map/while/body/eval_jaxpr/all_gather | solution.py:182
  436.8 182.3 %reduce-scatter.30.cloned.1.call-start = ((), (), s32[]{:S(2)}) async-start(), calls=%async_computation.23 | async-start | bytes 6684672 | tf_op jit(solution)/shard_map/while
  536.0 1.9 copy-start.2
  537.8 82.5 %copy-start.17 = (bf16[2,64,768]{1,2,0:T(8,128)(2,1)S(1)}, bf16[2,64,768]{1,2,0:T(8,128)(2,1)}, u32[]{:S(2)}) copy-start(bf16[2,64,768]{1,2,0:T(8,128)(2,1)} %get-tuple-element.498) | copy-start | bytes 589828 | tf_op jit(solution)/shard_map/while
  538.4 83.4 %copy-start.41 = (s32[2,64]{1,0:T(2,128)S(1)}, s32[2,64]{1,0:T(2,128)}, u32[]{:S(2)}) copy-start(s32[2,64]{1,0:T(2,128)} %copy-done.40) | copy-start | bytes 1540 | tf_op jit(solution)/shard_map/while
  621.8 5.3 copy-start.40
  621.8 43.3 %all-gather.50.cloned.1.call-start = ((), (), s32[]{:S(2)}) async-start(), calls=%async_computation.22 | async-start | bytes 1671168 | tf_op jit(solution)/shard_map/while/body/eval_jaxpr/all_gather | solution.py:183
  623.4 83.1 %all-gather.48.cloned.1.call-start = ((), (), s32[]{:S(2)}) async-start(), calls=%async_computation.21 | async-start | bytes 1671168 | tf_op jit(solution)/shard_map/while/body/eval_jaxpr/all_gather | solution.py:182
  625.0 181.8 %reduce-scatter.30.cloned.1.call-start = ((), (), s32[]{:S(2)}) async-start(), calls=%async_computation.23 | async-start | bytes 6684672 | tf_op jit(solution)/shard_map/while
  723.7 1.9 copy-start.2
  725.6 82.5 %copy-start.17 = (bf16[2,64,768]{1,2,0:T(8,128)(2,1)S(1)}, bf16[2,64,768]{1,2,0:T(8,128)(2,1)}, u32[]{:S(2)}) copy-start(bf16[2,64,768]{1,2,0:T(8,128)(2,1)} %get-tuple-element.498) | copy-start | bytes 589828 | tf_op jit(solution)/shard_map/while
  726.1 83.4 %copy-start.41 = (s32[2,64]{1,0:T(2,128)S(1)}, s32[2,64]{1,0:T(2,128)}, u32[]{:S(2)}) copy-start(s32[2,64]{1,0:T(2,128)} %copy-done.40) | copy-start | bytes 1540 | tf_op jit(solution)/shard_map/while
  809.5 77.9 %reduce-scatter.24.cloned.1.call-start = ((), (), s32[]{:S(2)}) async-start(), calls=%async_computation.16 | async-start | bytes 1769472
  812.7 76.2 %reduce-scatter.28.cloned.1.call-start = ((), (), s32[]{:S(2)}) async-start(), calls=%async_computation.18 | async-start | bytes 1769472
  814.7 75.5 %reduce-scatter.26.cloned.1.call-start = ((), (), s32[]{:S(2)}) async-start(), calls=%async_computation.17 | async-start | bytes 1769472
  816.9 92.0 %reduce-scatter.18.cloned.1.call-start = ((), (), s32[]{:S(2)}) async-start(), calls=%async_computation.13 | async-start | bytes 1769472 | tf_op jit(solution)/shard_map/reduce_scatter | solution.py:279
  818.5 153.4 %reduce-scatter.20.cloned.1.call-start = ((), (), s32[]{:S(2)}) async-start(), calls=%async_computation.14 | async-start | bytes 7077888 | tf_op jit(solution)/shard_map/reduce_scatter | solution.py:291
  822.3 212.6 %reduce-scatter.22.cloned.1.call-start = ((), (), s32[]{:S(2)}) async-start(), calls=%async_computation.15 | async-start | bytes 7077888 | tf_op jit(solution)/shard_map/reduce_scatter | solution.py:297
  827.1 48.6 %copy-start.36 = (bf16[768]{0:T(1024)(128)(2,1)S(1)}, bf16[768]{0:T(1024)(128)(2,1)}, u32[]{:S(2)}) copy-start(bf16[768]{0:T(1024)(128)(2,1)} %get-tuple-element.217) | copy-start | bytes 4612
  827.1 48.6 %copy-start.37 = (bf16[768]{0:T(1024)(128)(2,1)S(1)}, bf16[768]{0:T(1024)(128)(2,1)}, u32[]{:S(2)}) copy-start(bf16[768]{0:T(1024)(128)(2,1)} %get-tuple-element.221) | copy-start | bytes 4612
  827.1 48.6 %copy-start.38 = (bf16[768]{0:T(1024)(128)(2,1)S(1)}, bf16[768]{0:T(1024)(128)(2,1)}, u32[]{:S(2)}) copy-start(bf16[768]{0:T(1024)(128)(2,1)} %get-tuple-element.286) | copy-start | bytes 4612
  827.1 48.6 %copy-start.39 = (bf16[768]{0:T(1024)(128)(2,1)S(1)}, bf16[768]{0:T(1024)(128)(2,1)}, u32[]{:S(2)}) copy-start(bf16[768]{0:T(1024)(128)(2,1)} %get-tuple-element.219) | copy-start | bytes 4612
  827.1 56.7 %copy-start.13 = (bf16[768,768]{1,0:T(8,128)(2,1)S(1)}, bf16[768,768]{1,0:T(8,128)(2,1)}, u32[]{:S(2)}) copy-start(bf16[768,768]{1,0:T(8,128)(2,1)} %all-gather.34.cloned.1.call-done) | copy-start | bytes 3538948
  827.1 56.6 %copy-start.16 = (f32[128,768]{1,0:T(8,128)S(1)}, f32[128,768]{1,0:T(8,128)}, u32[]{:S(2)}) copy-start(f32[128,768]{1,0:T(8,128)} %copy-done.15) | copy-start | bytes 1179652
  873.7 11.2 copy-start.11
  873.7 11.2 copy-start.28
  1339.4 2.8 copy-start.25
  (21 other events, 27.4 us)
Sparse Core Ops, SparseCore 0:
  9.6 24.8 all-gather.35
  36.0 22.7 all-gather.33
  60.4 22.7 all-gather.31
  88.9 40.0 all-gather.45
  131.7 38.5 all-gather.43
  180.1 38.5 all-gather.45
  221.6 38.5 all-gather.43
  269.1 21.3 all-gather.37
  292.0 63.5 all-gather.39
  357.0 62.4 all-gather.41
  437.3 40.1 all-gather.49
  480.1 38.5 all-gather.47
  536.1 82.9 reduce-scatter.29
  625.2 39.9 all-gather.49
  667.9 38.5 all-gather.47
  723.8 82.9 reduce-scatter.29
  812.8 21.6 reduce-scatter.23
  837.3 21.8 reduce-scatter.27
  861.9 22.0 reduce-scatter.25
  886.8 22.0 reduce-scatter.17
  911.8 59.9 reduce-scatter.19
  974.8 59.9 reduce-scatter.21
where the time goes:
time: 1360 us; the launch traced here: 1350 us
  waiting for transfers between devices  738 us (54%)
  blocking collectives  423 us (31%)
  local copies, waits for them, and re-layouts  88.5 us (7%)
  matrix products  62.4 us (5%)
  other arithmetic  20 us (1%)
  between operations  19.5 us (1%)
    psum x1, blocking collectives, per_device(): lax.psum((grad_w_query, grad_b_query, grad_w_key, grad_w_value, grad_b_va...  305 us
    while x12, waiting for transfers between devices  160 us
    psum x2, blocking collectives, per_device(): lax.psum((jnp.sum(valid * error * error), jnp.sum(valid)), ('batch', 'ctx'))  78.7 us
    all_gather x2, waiting for transfers between devices, attend_forward(): lax.all_gather(key_one, 'ctx', axis=0, tiled=True)  75.3 us
    all_gather x2, waiting for transfers between devices, attend_backward(): lax.all_gather(value_one, 'ctx', axis=0, tiled=True)  73.7 us
    all_gather x2, waiting for transfers between devices, attend_backward(): lax.all_gather(key_one, 'ctx', axis=0, tiled=True)  73.4 us
    all_gather x2, waiting for transfers between devices, attend_forward(): lax.all_gather(value_one, 'ctx', axis=0, tiled=True)  71.5 us
    reduce_scatter x1, waiting for transfers between devices, per_device(): lax.psum_scatter(grad_w_outer.astype(jnp.bfloat16), 'batch', scatter_dime...  63 us
  transfers between devices with their start and end apart: 22, of which 18 were waited for; matrix products, arithmetic and copies ran while one was open for 6% of the time, Pallas kernels for 0%

commit v1 on v0

--- a/solution.py
+++ b/solution.py
@@ -2,6 +2,7 @@
 import jax.numpy as jnp
 from jax import lax
 from jax.sharding import PartitionSpec as P
+from jax.lax import psum
 
 H = 12
 HD = 64
@@ -152,8 +153,8 @@
     output, back_two = jax.vjp(norm_rows, hidden_two, gain_two_full, shift_two_full)
     valid = (seg_own.reshape(rows_here) != 0).astype(jnp.float32)[:, None]
     error = output - teacher.reshape(rows_here, width)
-    loss_total, valid_count = lax.psum(
-        (jnp.sum(valid * error * error), jnp.sum(valid)), ("batch", "ctx")
+    loss_total, valid_count = psum(
+        psum((jnp.sum(valid * error * error), jnp.sum(valid)), axis_name="batch"), axis_name="ctx"
     )
     loss = loss_total / (2.0 * valid_count)
     grad_output = tokens_all / valid_count * valid * error

time: 1360 us -> 1350 us (level)
  blocking collectives: 423 us -> 383 us
  waiting for transfers between devices: 738 us -> 778 us
    psum x3 -> x4, blocking collectives: 383 us -> 344 us  [the longest x2 335 us: per_device(): psum(psum((jnp.sum(valid * error * error), jnp.sum(valid)), axis_name='ba...]
    unnamed x15, waiting for transfers between devices: 4.14 us -> 34.6 us
  transfers between devices with their start and end apart: 22 -> 22, of which waited for: 18 -> 20; matrix products, arithmetic and copies ran while one was open for 6% -> 6% of each run, Pallas kernels for 0% -> 0%
where the time goes in v1:
time: 1350 us
  waiting for transfers between devices  778 us (58%)
  blocking collectives  383 us (28%)
  local copies, waits for them, and re-layouts  88.4 us (7%)
  matrix products  62.4 us (5%)
  other arithmetic  20.1 us (1%)
  between operations  19.4 us (1%)
    psum x2, blocking collectives, per_device(): psum(psum((jnp.sum(valid * error * error), jnp.sum(valid)), axis_name='ba...  335 us
    while x12, waiting for transfers between devices  160 us
    all_gather x2, waiting for transfers between devices, attend_forward(): lax.all_gather(key_one, 'ctx', axis=0, tiled=True)  75.3 us
    all_gather x2, waiting for transfers between devices, attend_backward(): lax.all_gather(value_one, 'ctx', axis=0, tiled=True)  73.7 us
    all_gather x2, waiting for transfers between devices, attend_backward(): lax.all_gather(key_one, 'ctx', axis=0, tiled=True)  73.4 us
    all_gather x2, waiting for transfers between devices, attend_forward(): lax.all_gather(value_one, 'ctx', axis=0, tiled=True)  71.5 us
    reduce_scatter x1, waiting for transfers between devices, per_device(): lax.psum_scatter(grad_w_outer.astype(jnp.bfloat16), 'batch', scatter_dime...  63 us
    reduce_scatter x1, waiting for transfers between devices, per_device(): lax.psum_scatter(grad_w_inner.astype(jnp.bfloat16), 'batch', scatter_dime...  62.9 us
  transfers between devices with their start and end apart: 22, of which 20 were waited for; matrix products, arithmetic and copies ran while one was open for 6% of the time, Pallas kernels for 0%

profile of v1, /device:TPU:1, one launch (start us, length us, event | category | flops | bytes accessed | tf_op | source)
XLA Modules:
  0.0 1352.8 jit_solution(13751252796342598220)
XLA Ops:
  9.5 3.7 all-gather.5
  13.3 3.2 all-gather.4
  17.3 17.2 %all-gather.36.cloned.1.call-done = bf16[768,768]{1,0:T(8,128)(2,1)} async-done(((bf16[384,768]{1,0:T(8,128)(2,1)}), bf16[768,768]{1,0:T(8,128)(2,1)}) %all-gather.36.cloned.1.call-update) | async-done | bytes 1179664 | tf_op jit(solution)/shard_map/all_gather | solution.py:88
  34.5 2.3 convolution_convert_fusion.4
  36.8 22.1 %all-gather.34.cloned.1.call-done = bf16[768,768]{1,0:T(8,128)(2,1)} async-done(((bf16[384,768]{1,0:T(8,128)(2,1)}), bf16[768,768]{1,0:T(8,128)(2,1)}) %all-gather.34.cloned.1.call-update) | async-done | bytes 1179664 | tf_op jit(solution)/shard_map/all_gather | solution.py:86
  58.8 2.3 fusion.27
  61.1 22.1 %all-gather.32.cloned.1.call-done = bf16[768,768]{1,0:T(8,128)(2,1)} async-done(((bf16[384,768]{1,0:T(8,128)(2,1)}), bf16[768,768]{1,0:T(8,128)(2,1)}) %all-gather.32.cloned.1.call-update) | async-done | bytes 1179664 | tf_op jit(solution)/shard_map/all_gather | solution.py:89
  83.2 2.3 fusion.26
  85.5 181.2 %while.26 = (s32[]{:T(128)}, bf16[2,64,768]{2,1,0:T(8,128)(2,1)}, f32[2,12,64]{2,1,0:T(8,128)}, bf16[2,64,768]{2,1,0:T(8,128)(2,1)}, s32[2,64]{1,0:T(2,128)S(1)}...) while((s32[]{:T(128)}, bf16[2,64,768]{2,1,0:T(8,128)(2,1)}, ...), condition=%wide.region_3.4_spmd, body=%wide.region_0.3_spmd.sunk | while | flops 210877696 | bytes 30582736 | solution.py:138
  90.6 38.4 %all-gather.46.cloned.1.call-done = bf16[1,1024,768]{2,1,0:T(8,128)(2,1)} async-done(((bf16[1,64,768]{2,1,0:T(8,128)(2,1)}), bf16[1,1024,768]{2,1,0:T(8,128)(2,1)}) %all-gather.46.cloned.1.call-update) | async-done | bytes 1572880 | tf_op jit(solution)/shard_map/while/body/eval_jaxpr/all_gather | solution.py:119
  129.0 2.6 copy.122
  131.6 2.2 fusion.113
  134.6 35.7 %all-gather.44.cloned.1.call-done = bf16[1,1024,768]{2,1,0:T(8,128)(2,1)} async-done(((bf16[1,64,768]{2,1,0:T(8,128)(2,1)}), bf16[1,1024,768]{2,1,0:T(8,128)(2,1)}) %all-gather.44.cloned.1.call-update) | async-done | bytes 1572880 | tf_op jit(solution)/shard_map/while/body/eval_jaxpr/all_gather | solution.py:120
  170.3 2.6 copy.121
  172.9 2.5 fusion.115
  181.9 36.9 %all-gather.46.cloned.1.call-done = bf16[1,1024,768]{2,1,0:T(8,128)(2,1)} async-done(((bf16[1,64,768]{2,1,0:T(8,128)(2,1)}), bf16[1,1024,768]{2,1,0:T(8,128)(2,1)}) %all-gather.46.cloned.1.call-update) | async-done | bytes 1572880 | tf_op jit(solution)/shard_map/while/body/eval_jaxpr/all_gather | solution.py:119
  218.7 2.6 copy.122
  221.3 2.2 fusion.113
  224.4 35.8 %all-gather.44.cloned.1.call-done = bf16[1,1024,768]{2,1,0:T(8,128)(2,1)} async-done(((bf16[1,64,768]{2,1,0:T(8,128)(2,1)}), bf16[1,1024,768]{2,1,0:T(8,128)(2,1)}) %all-gather.44.cloned.1.call-update) | async-done | bytes 1572880 | tf_op jit(solution)/shard_map/while/body/eval_jaxpr/all_gather | solution.py:120
  260.2 2.6 copy.121
  262.8 2.5 fusion.115
  269.4 4.4 psum.135
  273.9 30.8 %psum.136 = f32[]{:T(128)} all-reduce(f32[]{:T(128)} %psum.135), channel_id=1, replica_groups=mesh['batch'=2,'ctx'=16] {'ctx'}, use_global_device_ids=true, to_apply=%region_13.14 | all-reduce | flops 1 | bytes 8 | tf_op jit(solution)/shard_map/psum | solution.py:156
  304.7 3.5 all-gather.6
  308.3 3.5 all-gather.7
  311.8 3.5 all-gather.8
  315.4 3.5 all-gather.10
  319.0 3.5 all-gather.11
  322.5 3.5 all-gather.12
  327.0 3.8 all-gather.9
  332.8 22.1 %all-gather.40.cloned.1.call-done = bf16[768,3072]{1,0:T(8,128)(2,1)} async-done(((bf16[384,3072]{1,0:T(8,128)(2,1)}), bf16[768,3072]{1,0:T(8,128)(2,1)}) %all-gather.40.cloned.1.call-update) | async-done | bytes 4718608 | tf_op jit(solution)/shard_map/all_gather | solution.py:95
  354.9 7.6 multiply_convert_fusion.1
  362.5 56.5 %all-gather.42.cloned.1.call-done = bf16[3072,768]{1,0:T(8,128)(2,1)} async-done(((bf16[1536,768]{1,0:T(8,128)(2,1)}), bf16[3072,768]{1,0:T(8,128)(2,1)}) %all-gather.42.cloned.1.call-update) | async-done | bytes 4718608 | tf_op jit(solution)/shard_map/all_gather | solution.py:97
  419.0 3.4 fusion.45
  425.3 2.5 fusion.39
  427.8 2.4 multiply_reduce_fusion.2
  433.1 376.0 %while.27 = (s32[]{:T(128)}, bf16[2,64,768]{1,2,0:T(8,128)(2,1)}, bf16[2,64,768]{1,2,0:T(8,128)(2,1)}, bf16[2,64,768]{1,2,0:T(8,128)(2,1)}, bf16[2,64,768]{2,1,0...) while((s32[]{:T(128)}, bf16[2,64,768]{1,2,0:T(8,128)(2,1)}, ...), condition=%wide.region_21.22_spmd, body=%wide.region_18.21_spmd.sunk | while | flops 512916736 | bytes 120094944 | solution.py:230
  439.9 37.1 %all-gather.50.cloned.1.call-done = bf16[1,1024,768]{2,1,0:T(8,128)(2,1)} async-done(((bf16[1,64,768]{2,1,0:T(8,128)(2,1)}), bf16[1,1024,768]{2,1,0:T(8,128)(2,1)}) %all-gather.50.cloned.1.call-update) | async-done | bytes 1572880 | tf_op jit(solution)/shard_map/while/body/eval_jaxpr/all_gather | solution.py:184
  476.9 2.6 copy.126
  481.5 36.7 %all-gather.48.cloned.1.call-done = bf16[1,1024,768]{2,1,0:T(8,128)(2,1)} async-done(((bf16[1,64,768]{2,1,0:T(8,128)(2,1)}), bf16[1,1024,768]{2,1,0:T(8,128)(2,1)}) %all-gather.48.cloned.1.call-update) | async-done | bytes 1572880 | tf_op jit(solution)/shard_map/while/body/eval_jaxpr/all_gather | solution.py:183
  518.2 2.6 copy.124
  520.8 2.8 multiply_reduce_fusion.9
  525.7 3.2 pad_maximum_fusion.2
  528.9 6.6 copy.128
  538.6 80.0 %reduce-scatter.30.cloned.1.call-done = f32[64,1536]{1,0:T(8,128)} async-done(((f32[1024,1536]{1,0:T(8,128)}), f32[64,1536]{1,0:T(8,128)}) %reduce-scatter.30.cloned.1.call-update) | async-done | bytes 393232 | tf_op jit(solution)/shard_map/while
  628.1 36.6 %all-gather.50.cloned.1.call-done = bf16[1,1024,768]{2,1,0:T(8,128)(2,1)} async-done(((bf16[1,64,768]{2,1,0:T(8,128)(2,1)}), bf16[1,1024,768]{2,1,0:T(8,128)(2,1)}) %all-gather.50.cloned.1.call-update) | async-done | bytes 1572880 | tf_op jit(solution)/shard_map/while/body/eval_jaxpr/all_gather | solution.py:184
  664.7 2.6 copy.126
  669.3 36.7 %all-gather.48.cloned.1.call-done = bf16[1,1024,768]{2,1,0:T(8,128)(2,1)} async-done(((bf16[1,64,768]{2,1,0:T(8,128)(2,1)}), bf16[1,1024,768]{2,1,0:T(8,128)(2,1)}) %all-gather.48.cloned.1.call-update) | async-done | bytes 1572880 | tf_op jit(solution)/shard_map/while/body/eval_jaxpr/all_gather | solution.py:183
  706.0 2.6 copy.124
  708.6 2.8 multiply_reduce_fusion.9
  713.4 3.2 pad_maximum_fusion.2
  716.6 6.6 copy.128
  726.4 80.0 %reduce-scatter.30.cloned.1.call-done = f32[64,1536]{1,0:T(8,128)} async-done(((f32[1024,1536]{1,0:T(8,128)}), f32[64,1536]{1,0:T(8,128)}) %reduce-scatter.30.cloned.1.call-update) | async-done | bytes 393232 | tf_op jit(solution)/shard_map/while
  818.2 3.7 convolution_convert_fusion.1
  823.0 3.6 convolution_convert_fusion
  829.8 4.3 psum.133
  838.9 7.3 all-reduce.10
  851.7 7.3 reduce-scatter.28.cloned.1.call-done
  860.4 23.2 %reduce-scatter.26.cloned.1.call-done = bf16[384,768]{1,0:T(8,128)(2,1)} async-done(((bf16[768,768]{1,0:T(8,128)(2,1)}), bf16[384,768]{1,0:T(8,128)(2,1)}) %reduce-scatter.26.cloned.1.call-update) | async-done | bytes 589840
  885.0 23.2 %reduce-scatter.18.cloned.1.call-done = bf16[384,768]{1,0:T(8,128)(2,1)} async-done(((bf16[768,768]{1,0:T(8,128)(2,1)}), bf16[384,768]{1,0:T(8,128)(2,1)}) %reduce-scatter.18.cloned.1.call-update) | async-done | bytes 589840 | tf_op jit(solution)/shard_map/reduce_scatter | solution.py:280
  908.2 62.9 %reduce-scatter.20.cloned.1.call-done = bf16[384,3072]{1,0:T(8,128)(2,1)} async-done(((bf16[768,3072]{1,0:T(8,128)(2,1)}), bf16[384,3072]{1,0:T(8,128)(2,1)}) %reduce-scatter.20.cloned.1.call-update) | async-done | bytes 2359312 | tf_op jit(solution)/shard_map/reduce_scatter | solution.py:292
  971.1 63.0 %reduce-scatter.22.cloned.1.call-done = bf16[1536,768]{1,0:T(8,128)(2,1)} async-done(((bf16[3072,768]{1,0:T(8,128)(2,1)}), bf16[1536,768]{1,0:T(8,128)(2,1)}) %reduce-scatter.22.cloned.1.call-update) | async-done | bytes 2359312 | tf_op jit(solution)/shard_map/reduce_scatter | solution.py:298
  1034.1 304.6 %all-reduce.12 = (f32[]{:T(128)}, f32[384,768]{0,1:T(8,128)}, f32[384]{0:T(512)}, f32[384,768]{0,1:T(8,128)}, f32[384,768]{0,1:T(8,128)S(1)}, /*index=5*/f32[384...) all-reduce(f32[]{:T(128)} %psum.133, ...), channel_id=1, replica_groups=mesh['batch'=2,'ctx'=16] {'ctx'}, use_global_device_ids=true, to_apply=%region_10.11 | all-reduce | flops 3543553 | bytes 21270536 | tf_op jit(solution)/shard_map/psum | solution.py:156
  1338.7 2.7 copy.83
  (309 shorter events, 88.3 us)
Async XLA Ops:
  7.2 2.3 copy-start.44
  7.2 6.1 copy-start.45
  7.2 10.0 copy-start.5
  7.2 27.3 %all-gather.36.cloned.1.call-start = ((), (), s32[]{:S(2)}) async-start(), calls=%async_computation.9 | async-start | bytes 1769472 | tf_op jit(solution)/shard_map/all_gather | solution.py:88
  8.0 50.9 %all-gather.34.cloned.1.call-start = ((), (), s32[]{:S(2)}) async-start(), calls=%async_computation.8 | async-start | bytes 1769472 | tf_op jit(solution)/shard_map/all_gather | solution.py:86
  8.7 74.5 %all-gather.32.cloned.1.call-start = ((), (), s32[]{:S(2)}) async-start(), calls=%async_computation.7 | async-start | bytes 1769472 | tf_op jit(solution)/shard_map/all_gather | solution.py:89
  85.5 43.5 %all-gather.46.cloned.1.call-start = ((), (), s32[]{:S(2)}) async-start(), calls=%async_computation.20 | async-start | bytes 1671168 | tf_op jit(solution)/shard_map/while/body/eval_jaxpr/all_gather | solution.py:119
  87.1 83.2 %all-gather.44.cloned.1.call-start = ((), (), s32[]{:S(2)}) async-start(), calls=%async_computation.19 | async-start | bytes 1671168 | tf_op jit(solution)/shard_map/while/body/eval_jaxpr/all_gather | solution.py:120
  176.8 42.0 %all-gather.46.cloned.1.call-start = ((), (), s32[]{:S(2)}) async-start(), calls=%async_computation.20 | async-start | bytes 1671168 | tf_op jit(solution)/shard_map/while/body/eval_jaxpr/all_gather | solution.py:119
  178.3 81.8 %all-gather.44.cloned.1.call-start = ((), (), s32[]{:S(2)}) async-start(), calls=%async_computation.19 | async-start | bytes 1671168 | tf_op jit(solution)/shard_map/while/body/eval_jaxpr/all_gather | solution.py:120
  266.7 64.1 %all-gather.38.cloned.1.call-start = ((), (), s32[]{:S(2)}) async-start(), calls=%async_computation.10 | async-start | bytes 1769472 | tf_op jit(solution)/shard_map/all_gather | solution.py:91
  267.4 87.5 %all-gather.40.cloned.1.call-start = ((), (), s32[]{:S(2)}) async-start(), calls=%async_computation.11 | async-start | bytes 7077888 | tf_op jit(solution)/shard_map/all_gather | solution.py:95
  268.2 36.6 %copy-start.46 = (bf16[384]{0:T(512)(128)(2,1)S(1)}, bf16[384]{0:T(512)(128)(2,1)}, u32[]{:S(2)}) copy-start(bf16[384]{0:T(512)(128)(2,1)} %param.31) | copy-start | bytes 2308
  268.2 40.1 %copy-start.47 = (bf16[384]{0:T(512)(128)(2,1)S(1)}, bf16[384]{0:T(512)(128)(2,1)}, u32[]{:S(2)}) copy-start(bf16[384]{0:T(512)(128)(2,1)} %param.32) | copy-start | bytes 2308
  268.2 43.6 %copy-start.48 = (bf16[384]{0:T(512)(128)(2,1)S(1)}, bf16[384]{0:T(512)(128)(2,1)}, u32[]{:S(2)}) copy-start(bf16[384]{0:T(512)(128)(2,1)} %param.33) | copy-start | bytes 2308
  268.2 47.2 %copy-start.49 = (bf16[384]{0:T(512)(128)(2,1)S(1)}, bf16[384]{0:T(512)(128)(2,1)}, u32[]{:S(2)}) copy-start(bf16[384]{0:T(512)(128)(2,1)} %param.37) | copy-start | bytes 2308
  268.2 50.8 %copy-start.50 = (bf16[384]{0:T(512)(128)(2,1)S(1)}, bf16[384]{0:T(512)(128)(2,1)}, u32[]{:S(2)}) copy-start(bf16[384]{0:T(512)(128)(2,1)} %param.38) | copy-start | bytes 2308
  268.2 54.3 %copy-start.51 = (bf16[384]{0:T(512)(128)(2,1)S(1)}, bf16[384]{0:T(512)(128)(2,1)}, u32[]{:S(2)}) copy-start(bf16[384]{0:T(512)(128)(2,1)} %param.39) | copy-start | bytes 2308
  268.2 58.7 %copy-start.42 = (bf16[1536]{0:T(1024)(128)(2,1)S(1)}, bf16[1536]{0:T(1024)(128)(2,1)}, u32[]{:S(2)}) copy-start(bf16[1536]{0:T(1024)(128)(2,1)} %param.35) | copy-start | bytes 9220
  268.2 62.6 %copy-start.6 = (f32[2,64,768]{2,1,0:T(8,128)S(1)}, f32[2,64,768]{2,1,0:T(8,128)}, u32[]{:S(2)}) copy-start(f32[2,64,768]{2,1,0:T(8,128)} %param.22) | copy-start | bytes 1179652
  268.2 62.6 %copy-start.26 = (bf16[2,64,768]{2,1,0:T(8,128)(2,1)S(1)}, bf16[2,64,768]{2,1,0:T(8,128)(2,1)}, u32[]{:S(2)}) copy-start(bf16[2,64,768]{2,1,0:T(8,128)(2,1)} %get-tuple-element.120) | copy-start | bytes 589828
  268.3 150.7 %all-gather.42.cloned.1.call-start = ((), (), s32[]{:S(2)}) async-start(), calls=%async_computation.12 | async-start | bytes 7077888 | tf_op jit(solution)/shard_map/all_gather | solution.py:97
  332.5 97.6 %copy-start.3 = (f32[128,768]{1,0:T(8,128)}, f32[128,768]{1,0:T(8,128)S(1)}, u32[]{:S(2)}) copy-start(f32[128,768]{1,0:T(8,128)S(1)} %get-tuple-element.312) | copy-start | bytes 1179652
  332.6 97.6 %copy-start.32 = (f32[128]{0:T(128)}, f32[128]{0:T(128)S(1)}, u32[]{:S(2)}) copy-start(f32[128]{0:T(128)S(1)} %broadcast_multiply_fusion.1) | copy-start | bytes 1540
  332.8 97.4 %copy-start.34 = (f32[128]{0:T(128)}, f32[128]{0:T(128)S(1)}, u32[]{:S(2)}) copy-start(f32[128]{0:T(128)S(1)} %fusion.30) | copy-start | bytes 1540
  362.5 59.9 %copy-start.8 = (bf16[128,3072]{1,0:T(8,128)(2,1)}, bf16[128,3072]{1,0:T(8,128)(2,1)S(1)}, u32[]{:S(2)}) copy-start(bf16[128,3072]{1,0:T(8,128)(2,1)S(1)} %get-tuple-element.301) | copy-start | bytes 2359300
  419.0 3.6 copy-start.31
  419.0 6.3 copy-start.10
  422.6 2.7 copy-start.53
  424.3 3.5 slice-start
  425.3 2.5 copy-start.29
  425.3 2.5 slice-start.1
  427.8 2.4 copy-start.20
  430.1 1.7 copy-start.14
  430.4 2.7 copy-start.43
  433.1 5.3 copy-start.40
  433.1 43.8 %all-gather.50.cloned.1.call-start = ((), (), s32[]{:S(2)}) async-start(), calls=%async_computation.22 | async-start | bytes 1671168 | tf_op jit(solution)/shard_map/while/body/eval_jaxpr/all_gather | solution.py:184
  434.7 83.5 %all-gather.48.cloned.1.call-start = ((), (), s32[]{:S(2)}) async-start(), calls=%async_computation.21 | async-start | bytes 1671168 | tf_op jit(solution)/shard_map/while/body/eval_jaxpr/all_gather | solution.py:183
  436.3 182.3 %reduce-scatter.30.cloned.1.call-start = ((), (), s32[]{:S(2)}) async-start(), calls=%async_computation.23 | async-start | bytes 6684672 | tf_op jit(solution)/shard_map/while
  535.5 1.9 copy-start.2
  537.3 82.5 %copy-start.17 = (bf16[2,64,768]{1,2,0:T(8,128)(2,1)S(1)}, bf16[2,64,768]{1,2,0:T(8,128)(2,1)}, u32[]{:S(2)}) copy-start(bf16[2,64,768]{1,2,0:T(8,128)(2,1)} %get-tuple-element.499) | copy-start | bytes 589828 | tf_op jit(solution)/shard_map/while
  537.9 83.4 %copy-start.41 = (s32[2,64]{1,0:T(2,128)S(1)}, s32[2,64]{1,0:T(2,128)}, u32[]{:S(2)}) copy-start(s32[2,64]{1,0:T(2,128)} %copy-done.40) | copy-start | bytes 1540 | tf_op jit(solution)/shard_map/while
  621.3 5.3 copy-start.40
  621.3 43.4 %all-gather.50.cloned.1.call-start = ((), (), s32[]{:S(2)}) async-start(), calls=%async_computation.22 | async-start | bytes 1671168 | tf_op jit(solution)/shard_map/while/body/eval_jaxpr/all_gather | solution.py:184
  622.9 83.1 %all-gather.48.cloned.1.call-start = ((), (), s32[]{:S(2)}) async-start(), calls=%async_computation.21 | async-start | bytes 1671168 | tf_op jit(solution)/shard_map/while/body/eval_jaxpr/all_gather | solution.py:183
  624.5 181.9 %reduce-scatter.30.cloned.1.call-start = ((), (), s32[]{:S(2)}) async-start(), calls=%async_computation.23 | async-start | bytes 6684672 | tf_op jit(solution)/shard_map/while
  723.2 1.9 copy-start.2
  725.1 82.5 %copy-start.17 = (bf16[2,64,768]{1,2,0:T(8,128)(2,1)S(1)}, bf16[2,64,768]{1,2,0:T(8,128)(2,1)}, u32[]{:S(2)}) copy-start(bf16[2,64,768]{1,2,0:T(8,128)(2,1)} %get-tuple-element.499) | copy-start | bytes 589828 | tf_op jit(solution)/shard_map/while
  725.7 83.4 %copy-start.41 = (s32[2,64]{1,0:T(2,128)S(1)}, s32[2,64]{1,0:T(2,128)}, u32[]{:S(2)}) copy-start(s32[2,64]{1,0:T(2,128)} %copy-done.40) | copy-start | bytes 1540 | tf_op jit(solution)/shard_map/while
  809.1 41.3 %reduce-scatter.24.cloned.1.call-start = ((), (), s32[]{:S(2)}) async-start(), calls=%async_computation.16 | async-start | bytes 1769472
  812.2 46.8 %reduce-scatter.28.cloned.1.call-start = ((), (), s32[]{:S(2)}) async-start(), calls=%async_computation.18 | async-start | bytes 1769472
  814.3 69.3 %reduce-scatter.26.cloned.1.call-start = ((), (), s32[]{:S(2)}) async-start(), calls=%async_computation.17 | async-start | bytes 1769472
  816.5 91.7 %reduce-scatter.18.cloned.1.call-start = ((), (), s32[]{:S(2)}) async-start(), calls=%async_computation.13 | async-start | bytes 1769472 | tf_op jit(solution)/shard_map/reduce_scatter | solution.py:280
  818.1 153.0 %reduce-scatter.20.cloned.1.call-start = ((), (), s32[]{:S(2)}) async-start(), calls=%async_computation.14 | async-start | bytes 7077888 | tf_op jit(solution)/shard_map/reduce_scatter | solution.py:292
  821.9 212.2 %reduce-scatter.22.cloned.1.call-start = ((), (), s32[]{:S(2)}) async-start(), calls=%async_computation.15 | async-start | bytes 7077888 | tf_op jit(solution)/shard_map/reduce_scatter | solution.py:298
  826.6 12.2 copy-start.36
  826.7 12.2 copy-start.37
  826.7 12.2 copy-start.38
  826.7 12.2 copy-start.39
  826.7 19.9 %copy-start.13 = (bf16[768,768]{1,0:T(8,128)(2,1)S(1)}, bf16[768,768]{1,0:T(8,128)(2,1)}, u32[]{:S(2)}) copy-start(bf16[768,768]{1,0:T(8,128)(2,1)} %all-gather.34.cloned.1.call-done) | copy-start | bytes 3538948
  826.7 19.9 %copy-start.16 = (f32[128,768]{1,0:T(8,128)S(1)}, f32[128,768]{1,0:T(8,128)}, u32[]{:S(2)}) copy-start(f32[128,768]{1,0:T(8,128)} %copy-done.15) | copy-start | bytes 1179652
  837.5 10.4 copy-start.11
  837.5 10.4 copy-start.28
  1338.7 2.8 copy-start.25
  (21 other events, 27.4 us)
Sparse Core Ops, SparseCore 0:
  9.6 24.8 all-gather.35
  36.0 22.7 all-gather.33
  60.4 22.7 all-gather.31
  88.9 40.0 all-gather.45
  131.7 38.5 all-gather.43
  180.1 38.5 all-gather.45
  221.6 38.5 all-gather.43
  269.0 21.2 all-gather.37
  291.9 62.9 all-gather.39
  356.3 62.6 all-gather.41
  436.8 40.1 all-gather.49
  479.6 38.5 all-gather.47
  535.6 82.9 reduce-scatter.29
  624.7 39.9 all-gather.49
  667.4 38.5 all-gather.47
  723.4 82.9 reduce-scatter.29
  812.4 21.5 reduce-scatter.23
  836.8 22.1 reduce-scatter.27
  861.9 21.7 reduce-scatter.25
  886.4 21.7 reduce-scatter.17
  911.0 59.9 reduce-scatter.19
  974.1 59.9 reduce-scatter.21
